TPU v7x, 32 devices: a whole 2x2x4 slice. The times are simulated.
32 devices in a mesh: donor: 16 (over z, y, x), gene: 2 (over core).
Axes of the slice: x: 2, y: 2, z: 4, core: 2. Of those that a mesh axis runs over, the one named last changes fastest.
Arguments:
- embeddings: bfloat16 [32768, 512], P('donor', 'gene')
- targets_by_gene: bfloat16 [5120, 32768], P(('gene', 'donor')), may hold values from -6 to 6
- cell_counts: int32 [16], P('donor'), may hold values from 1024 to 2048, as said below
Outputs:
- coefficients: float32 [512, 5120], P('donor', 'gene')
Inputs may be any that keep to these rules, and one draw needn't show every extreme that they name: `cell_counts`: every entry is a multiple of 128; some entry equals 2048 and some entry equals 2048/2.
All inputs are finite; a program needn't handle non-finite values.
Results may differ from a plain program's by a relative error of at most 0.0003.
Values may be sent and summed in bfloat16 or wider, within the bound.
No kernel may reach another device: no remote copies, remote signals or barrier semaphores. Data moves between devices by JAX's collectives and lax.ppermute only.
A program may use at most 128 MiB of HBM per device.

v0:
```python
import math
import jax
import jax.numpy as jnp
from jax import lax
from jax.sharding import PartitionSpec as P


def solve_both(lower_factor, right_cols):
    halfway = lax.linalg.triangular_solve(lower_factor, right_cols, left_side=True, lower=True)
    return lax.linalg.triangular_solve(
        lower_factor, halfway, left_side=True, lower=True, transpose_a=True
    )


def shards(embeddings, targets_by_gene, cell_counts):
    valid_count = cell_counts[0]
    gathered = lax.all_gather(embeddings, "gene", axis=1, tiled=True)
    row_total = gathered.shape[0]
    width = gathered.shape[1]
    donors = lax.axis_size("donor")
    row_valid = lax.broadcasted_iota(jnp.int32, (row_total, 1), 0) < valid_count
    masked = jnp.where(row_valid, gathered, jnp.zeros_like(gathered))
    gram_matrix = lax.dot_general(
        masked, masked, (((0,), (0,)), ((), ())), preferred_element_type=jnp.float32
    )
    by_rows = lax.all_to_all(targets_by_gene, "donor", split_axis=1, concat_axis=0, tiled=True)
    gram_matrix = lax.psum(gram_matrix, "donor")
    lower_factor = jnp.linalg.cholesky(gram_matrix)
    scale_total = math.sqrt(row_total * donors)
    cross_local = jnp.dot(by_rows, masked, preferred_element_type=jnp.float32)
    cross_sum = lax.psum(cross_local, "donor")
    scaled = scale_total * solve_both(lower_factor, cross_sum.T)
    share = width // donors
    first_row = lax.axis_index("donor") * share
    return lax.dynamic_slice_in_dim(scaled, first_row, share, 0)


def solution(mesh):
    placed = (P("donor", "gene"), P(("gene", "donor"), None), P("donor"))
    return jax.shard_map(
        shards, mesh=mesh, in_specs=placed, out_specs=P("donor", "gene"), check_vma=False
    )
```

profile of v0, /device:TPU:0, one launch (start us, length us, event | category | flops | bytes accessed | tf_op | source)
XLA Modules:
  0.0 653.4 jit_solution(13016904788041452031)
XLA Ops:
  6.5 10.0 %copy.17 = bf16[20,16,8,2048]{3,2,0,1:T(8,128)(2,1)} copy(bf16[20,16,8,2048]{3,2,1,0:T(8,128)(2,1)} %bitcast.68) | data formatting | bytes 20971520 | tf_op jit(solution)/shard_map/all_to_all | solution.py:26
  16.6 8.4 %all-to-all-start = ((bf16[160,16,2048]{2,0,1:T(8,128)(2,1)}), bf16[160,16,2048]{2,0,1:T(8,128)(2,1)}, u32[]{:S(2)}, u32[]{:S(2)}) async-start(bf16[160,16,2048]{2,0,1:T(8,128)(2,1)} %bitcast.67), calls=%async_computation | async-start | bytes 20971520 | tf_op jit(solution)/shard_map/all_to_all | solution.py:26
  24.9 0.0 all-gather.2.cloned.1.call-start
  25.0 0.7 all-gather.2.cloned.1.call-update
  25.7 0.0 all-reduce.4.cloned.1.call-start
  26.4 12.5 %all-gather.2.cloned.1.call-done = bf16[2048,512]{1,0:T(8,128)(2,1)} async-done(((bf16[2048,256]{1,0:T(8,128)(2,1)}), bf16[2048,512]{1,0:T(8,128)(2,1)}) %all-gather.2.cloned.1.call-update) | async-done | bytes 2097168 | tf_op jit(solution)/shard_map/all_gather | solution.py:17
  38.9 5.2 fusion.28
  44.1 178.5 %all-to-all-done = bf16[160,16,2048]{2,0,1:T(8,128)(2,1)} async-done(((bf16[160,16,2048]{2,0,1:T(8,128)(2,1)}), bf16[160,16,2048]{2,0,1:T(8,128)(2,1)}, u32[]{:S(2)}, u32[]{:S(2)}) %all-to-all-start) | async-done | bytes 10485792 | tf_op jit(solution)/shard_map/all_to_all | solution.py:26
  222.6 10.8 %fusion.27 = f32[512,2560]{1,0:T(8,128)} fusion(bf16[2560,2048]{1,0:T(8,128)(2,1)} %bitcast.10, bf16[2048,512]{1,0:T(8,128)(2,1)S(1)} %copy-done.1, pred[2048]{0:T(1024)(128)(4,1)S(1)} %iota_compare_fusion.3), kind=kOutput, calls=%fused_computation.43 | convolution fusion | flops 5369757696 | bytes 17827840 | tf_op jit(solution)/shard_map/dot_general | solution.py:30
  233.4 0.0 all-reduce.4.cloned.1.call-update
  233.5 251.7 %all-reduce.4.cloned.1.call-done = (f32[512,2560]{1,0:T(8,128)}, f32[512,512]{0,1:T(8,128)}) async-done(((f32[512,2560]{1,0:T(8,128)}, f32[512,512]{0,1:T(8,128)}), (f32[512,2560]{1,0:T(8,128)}, f32[512,512]{0,1:T(8,128)})) %all-reduce.4.cloned.1.call-update) | async-done | bytes 6291472 | tf_op jit(solution)/shard_map/psum | solution.py:31
  485.2 1.6 copy.12
  486.8 0.0 copy-done
  486.8 0.2 fusion.26
  487.1 11.7 %cholesky.104 = f32[128,128]{1,0:T(8,128)S(1)} custom-call(f32[128,128]{1,0:T(8,128)S(1)} %cholesky.266), custom_call_target="Cholesky" | custom-call | tf_op jit(solution)/shard_map/jit(cholesky)/cholesky | solution.py:28
  498.8 0.1 cholesky.224
  498.9 9.8 %custom-call.32 = f32[1,128,128]{1,2,0:T(8,128)S(1)} custom-call(f32[1,128,128]{2,1,0:T(8,128)S(1)} %get-tuple-element.34), custom_call_target="InvertDiagBlocksLowerTriangular" | custom-call | tf_op jit(solution)/shard_map/jit(cholesky)/cholesky | solution.py:28
  508.8 0.3 constant_dynamic-update-slice_fusion
  509.1 0.3 convolution_subtract_fusion.4
  509.4 11.7 %cholesky.217 = f32[128,128]{1,0:T(8,128)S(1)} custom-call(f32[128,128]{1,0:T(8,128)S(1)} %cholesky.270), custom_call_target="Cholesky" | custom-call | tf_op jit(solution)/shard_map/jit(cholesky)/cholesky | solution.py:28
  521.2 10.2 %custom-call.33 = f32[1,128,128]{1,2,0:T(8,128)S(1)} custom-call(f32[1,128,128]{2,1,0:T(8,128)S(1)} %get-tuple-element.31), custom_call_target="InvertDiagBlocksLowerTriangular" | custom-call | tf_op jit(solution)/shard_map/jit(cholesky)/cholesky | solution.py:28
  531.4 0.3 convolution_dynamic-update-slice_fusion
  531.6 0.0 slice-start
  531.6 0.4 convolution_subtract_fusion.5
  532.0 11.7 %cholesky.238 = f32[128,128]{1,0:T(8,128)S(1)} custom-call(f32[128,128]{1,0:T(8,128)S(1)} %cholesky.275), custom_call_target="Cholesky" | custom-call | tf_op jit(solution)/shard_map/jit(cholesky)/cholesky | solution.py:28
  543.8 9.8 %custom-call.34 = f32[1,128,128]{1,2,0:T(8,128)S(1)} custom-call(f32[1,128,128]{2,1,0:T(8,128)S(1)} %get-tuple-element.28), custom_call_target="InvertDiagBlocksLowerTriangular" | custom-call | tf_op jit(solution)/shard_map/jit(cholesky)/cholesky | solution.py:28
  553.6 0.2 convolution_dynamic-update-slice_fusion.1
  553.8 0.4 convolution_subtract_fusion.6
  554.2 11.7 %cholesky.255 = f32[128,128]{1,0:T(8,128)S(1)} custom-call(f32[128,128]{1,0:T(8,128)S(1)} %convolution_subtract_fusion.6), custom_call_target="Cholesky" | custom-call | tf_op jit(solution)/shard_map/jit(cholesky)/cholesky | solution.py:28
  566.0 0.7 compare_reduce_fusion.1
  566.6 0.7 compare_reduce_fusion
  567.3 0.7 compare_reduce_fusion.2
  570.6 0.3 select_select_fusion
  570.9 10.6 %while.1 = (s32[]{:T(128)}, f32[512,512]{1,0:T(8,128)S(1)}, s32[4,2]{0,1:T(2,128)S(1)}, f32[4,128,128]{2,1,0:T(8,128)}, s32[]{:T(128)}) while((s32[]{:T(128)}, f32[512,512]{1,0:T(8,128)S(1)}, s32[4,2]{0,1:T(2,128)S(1)}, f32[4,128,128]{2,1,0:T(8,128)}, s32[]{:T(128)}) %tuple.27), condition=%wide.while_cond, body=%wide.while_body.sunk | while | flops 2 | bytes 132205 | solution.py:10
  570.9 0.1 constant_dynamic-slice_fusion.2
  571.0 0.6 fusion.76
  571.6 2.0 bitcast_dynamic-update-slice_fusion.2
  573.5 0.1 constant_dynamic-slice_fusion.2
  573.6 0.6 fusion.76
  574.2 2.0 bitcast_dynamic-update-slice_fusion.2
  576.2 0.1 constant_dynamic-slice_fusion.2
  576.3 0.6 fusion.76
  576.8 2.0 bitcast_dynamic-update-slice_fusion.2
  578.8 0.1 constant_dynamic-slice_fusion.2
  578.9 0.6 fusion.76
  579.5 2.0 bitcast_dynamic-update-slice_fusion.2
  581.5 40.1 %custom-call.35 = f32[4,128,128]{1,2,0:T(8,128)S(1)} custom-call(f32[4,128,128]{2,1,0:T(8,128)} %get-tuple-element.12), custom_call_target="InvertDiagBlocksLowerTriangular" | custom-call | tf_op jit(solution)/shard_map/triangular_solve | solution.py:10
  621.6 0.0 slice-start.1
  621.6 2.7 fusion.24
  624.3 2.6 convolution_subtract_fusion.1
  626.9 1.3 fusion.52
  628.2 0.0 slice-done
  628.2 1.5 convolution_subtract_fusion.3
  629.8 1.3 fusion.54
  631.0 2.5 fusion.15
  633.5 1.3 fusion.56
  634.8 1.3 fusion.55
  636.1 1.5 convolution_subtract_fusion
  637.6 1.3 fusion.53
  638.9 1.6 convolution_subtract_fusion.2
  640.4 1.3 fusion.51
  641.7 2.5 fusion.12
  644.2 1.3 fusion.50
  645.5 0.8 fusion.32
  (16 shorter events, 0.2 us)
Async XLA Ops:
  16.6 206.0 %all-to-all-start = ((bf16[160,16,2048]{2,0,1:T(8,128)(2,1)}), bf16[160,16,2048]{2,0,1:T(8,128)(2,1)}, u32[]{:S(2)}, u32[]{:S(2)}) async-start(bf16[160,16,2048]{2,0,1:T(8,128)(2,1)} %bitcast.67), calls=%async_computation | async-start | bytes 20971520 | tf_op jit(solution)/shard_map/all_to_all | solution.py:26
  24.9 14.0 %all-gather.2.cloned.1.call-start = ((), (), s32[]{:S(2)}) async-start(), calls=%async_computation.1 | async-start | bytes 3145728 | tf_op jit(solution)/shard_map/all_gather | solution.py:17
  25.7 459.5 %all-reduce.4.cloned.1.call-start = ((), (), s32[]{:S(2)}) async-start(), calls=%async_computation.2 | async-start | bytes 12582912 | tf_op jit(solution)/shard_map/psum | solution.py:31
  38.9 183.7 %copy-start.1 = (bf16[2048,512]{1,0:T(8,128)(2,1)S(1)}, bf16[2048,512]{1,0:T(8,128)(2,1)}, u32[]{:S(2)}) copy-start(bf16[2048,512]{1,0:T(8,128)(2,1)} %all-gather.2.cloned.1.call-done) | copy-start | bytes 6291460
  485.2 1.7 copy-start
  531.6 96.5 %slice-start = ((s8[5242880]{0:T(1024)(128)(4,1)}), s8[1048576]{0:T(1024)(128)(4,1)S(1)}, s32[]{:S(2)}) async-start(s8[5242880]{0:T(1024)(128)(4,1)} %bitcast.69), calls=%async_computation.3 | async-start | bytes 2097152
  621.6 6.6 %slice-start.1 = ((s8[5242880]{0:T(1024)(128)(4,1)}), s8[4194304]{0:T(1024)(128)(4,1)S(1)}, s32[]{:S(2)}) async-start(s8[5242880]{0:T(1024)(128)(4,1)} %bitcast.69), calls=%async_computation.4 | async-start | bytes 8388608
Sparse Core Ops, SparseCore 0:
  27.3 11.5 all-gather.1
  233.6 251.5 all-reduce.3
where the time goes:
time: 659 us; the launch traced here: 653 us
  waiting for transfers between devices  443 us (67%)
  other arithmetic  120 us (18%)
  matrix products  41.6 us (6%)
  local copies, waits for them, and re-layouts  22.4 us (3%)
  between operations  17.2 us (3%)
  starting transfers between devices  8.44 us (1%)
    psum x1, waiting for transfers between devices, shards(): cross_sum = lax.psum(cross_local, 'donor')  252 us
    all_to_all x1, waiting for transfers between devices, shards(): lax.all_to_all(targets_by_gene, 'donor', split_axis=1, concat_axis=0, til...  178 us
    another operation x14, other arithmetic, shards(): lower_factor = jnp.linalg.cholesky(gram_matrix)  78.9 us
    another operation x3, other arithmetic, solve_both(): lax.linalg.triangular_solve(lower_factor, halfway, left_side=True, lower=...  40.4 us
  transfers between devices with their start and end apart: 3, of which 3 were waited for; matrix products, arithmetic and copies ran while one was open for 1% of the time, Pallas kernels for 0%

commit v1 on v0

--- a/solution.py
+++ b/solution.py
@@ -23,7 +23,12 @@
     gram_matrix = lax.dot_general(
         masked, masked, (((0,), (0,)), ((), ())), preferred_element_type=jnp.float32
     )
-    by_rows = lax.all_to_all(targets_by_gene, "donor", split_axis=1, concat_axis=0, tiled=True)
+    by_rows = jnp.concatenate(
+        lax.all_to_all(
+            jnp.stack(jnp.split(targets_by_gene, lax.axis_size("donor"), axis=1)), "donor", 0, 0
+        ),
+        axis=0,
+    )
     gram_matrix = lax.psum(gram_matrix, "donor")
     lower_factor = jnp.linalg.cholesky(gram_matrix)
     scale_total = math.sqrt(row_total * donors)

time: 659 us -> 681 us (1.033)
  local copies, waits for them, and re-layouts: 22.4 us -> 44.4 us
    unnamed x8 -> x23, local copies, waits for them, and re-layouts: 0.02 us -> 30 us
    all_to_all x1 -> x0, local copies, waits for them, and re-layouts: 10 us -> none  [shards(): lax.all_to_all(targets_by_gene, 'donor', split_axis=1, concat_axis=0, til...]
where the time goes in v1:
time: 681 us; the launch traced here: 675 us
  waiting for transfers between devices  443 us (65%)
  other arithmetic  120 us (18%)
  local copies, waits for them, and re-layouts  44.4 us (7%)
  matrix products  41.6 us (6%)
  between operations  17.2 us (3%)
  starting transfers between devices  8.44 us (1%)
    psum x1, waiting for transfers between devices, shards(): cross_sum = lax.psum(cross_local, 'donor')  252 us
    all_to_all x1, waiting for transfers between devices, shards(): lax.all_to_all(jnp.stack(jnp.split(targets_by_gene, lax.axis_size('donor'...  178 us
    another operation x14, other arithmetic, shards(): lower_factor = jnp.linalg.cholesky(gram_matrix)  78.9 us
    another operation x3, other arithmetic, solve_both(): lax.linalg.triangular_solve(lower_factor, halfway, left_side=True, lower=...  40.4 us
    unnamed x23, local copies, waits for them, and re-layouts  30 us
  transfers between devices with their start and end apart: 3, of which 3 were waited for; matrix products, arithmetic and copies ran while one was open for 1% of the time, Pallas kernels for 0%

profile of v1, /device:TPU:0, one launch (start us, length us, event | category | flops | bytes accessed | tf_op | source)
XLA Modules:
  0.0 675.4 jit_solution(8993087154338507687)
XLA Ops:
  6.5 2.0 bitcast_dynamic-update-slice_fusion.16
  8.5 2.0 bitcast_dynamic-update-slice_fusion.15
  10.5 2.0 bitcast_dynamic-update-slice_fusion.14
  12.5 2.0 bitcast_dynamic-update-slice_fusion.13
  14.5 2.0 bitcast_dynamic-update-slice_fusion.12
  16.5 2.0 bitcast_dynamic-update-slice_fusion.11
  18.5 2.0 bitcast_dynamic-update-slice_fusion.10
  20.5 2.0 bitcast_dynamic-update-slice_fusion.9
  22.5 2.0 bitcast_dynamic-update-slice_fusion.8
  24.5 2.0 bitcast_dynamic-update-slice_fusion.7
  26.5 2.0 bitcast_dynamic-update-slice_fusion.6
  28.5 2.0 bitcast_dynamic-update-slice_fusion.5
  30.5 2.0 bitcast_dynamic-update-slice_fusion.4
  32.5 2.0 bitcast_dynamic-update-slice_fusion.3
  34.5 2.0 bitcast_dynamic-update-slice_fusion.2
  36.5 2.0 bitcast_dynamic-update-slice_fusion.1
  38.5 8.4 %all-to-all-start = ((bf16[16,160,2048]{2,1,0:T(8,128)(2,1)}), bf16[16,160,2048]{2,1,0:T(8,128)(2,1)}, u32[]{:S(2)}, u32[]{:S(2)}) async-start(bf16[16,160,2048]{2,1,0:T(8,128)(2,1)} %bitcast_dynamic-update-slice_fusion.1), calls=%async_computation | async-start | bytes 20971520 | tf_op jit(solution)/shard_map/all_to_all | solution.py:27
  46.9 0.7 all-gather.2.cloned.1.call-update
  48.3 12.5 %all-gather.2.cloned.1.call-done = bf16[2048,512]{1,0:T(8,128)(2,1)} async-done(((bf16[2048,256]{1,0:T(8,128)(2,1)}), bf16[2048,512]{1,0:T(8,128)(2,1)}) %all-gather.2.cloned.1.call-update) | async-done | bytes 2097168 | tf_op jit(solution)/shard_map/all_gather | solution.py:17
  60.9 5.2 fusion.28
  66.1 178.5 %all-to-all-done = bf16[16,160,2048]{2,1,0:T(8,128)(2,1)} async-done(((bf16[16,160,2048]{2,1,0:T(8,128)(2,1)}), bf16[16,160,2048]{2,1,0:T(8,128)(2,1)}, u32[]{:S(2)}, u32[]{:S(2)}) %all-to-all-start) | async-done | bytes 10485792 | tf_op jit(solution)/shard_map/all_to_all | solution.py:27
  244.5 10.8 %fusion.27 = f32[512,2560]{1,0:T(8,128)} fusion(bf16[2560,2048]{1,0:T(8,128)(2,1)} %bitcast.25, bf16[2048,512]{1,0:T(8,128)(2,1)S(1)} %copy-done.1, pred[2048]{0:T(1024)(128)(4,1)S(1)} %iota_compare_fusion.3), kind=kOutput, calls=%fused_computation.42 | convolution fusion | flops 5369757696 | bytes 17827840 | tf_op jit(solution)/shard_map/dot_general | solution.py:35
  255.4 251.7 %all-reduce.4.cloned.1.call-done = (f32[512,2560]{1,0:T(8,128)}, f32[512,512]{0,1:T(8,128)}) async-done(((f32[512,2560]{1,0:T(8,128)}, f32[512,512]{0,1:T(8,128)}), (f32[512,2560]{1,0:T(8,128)}, f32[512,512]{0,1:T(8,128)})) %all-reduce.4.cloned.1.call-update) | async-done | bytes 6291472 | tf_op jit(solution)/shard_map/psum | solution.py:36
  507.1 1.6 copy.5
  509.0 11.7 %cholesky.104 = f32[128,128]{1,0:T(8,128)S(1)} custom-call(f32[128,128]{1,0:T(8,128)S(1)} %cholesky.266), custom_call_target="Cholesky" | custom-call | tf_op jit(solution)/shard_map/jit(cholesky)/cholesky | solution.py:33
  520.9 9.8 %custom-call.32 = f32[1,128,128]{1,2,0:T(8,128)S(1)} custom-call(f32[1,128,128]{2,1,0:T(8,128)S(1)} %get-tuple-element.34), custom_call_target="InvertDiagBlocksLowerTriangular" | custom-call | tf_op jit(solution)/shard_map/jit(cholesky)/cholesky | solution.py:33
  530.7 0.3 constant_dynamic-update-slice_fusion
  531.1 0.3 convolution_subtract_fusion.4
  531.4 11.7 %cholesky.217 = f32[128,128]{1,0:T(8,128)S(1)} custom-call(f32[128,128]{1,0:T(8,128)S(1)} %cholesky.270), custom_call_target="Cholesky" | custom-call | tf_op jit(solution)/shard_map/jit(cholesky)/cholesky | solution.py:33
  543.2 10.2 %custom-call.33 = f32[1,128,128]{1,2,0:T(8,128)S(1)} custom-call(f32[1,128,128]{2,1,0:T(8,128)S(1)} %get-tuple-element.31), custom_call_target="InvertDiagBlocksLowerTriangular" | custom-call | tf_op jit(solution)/shard_map/jit(cholesky)/cholesky | solution.py:33
  553.6 0.4 convolution_subtract_fusion.5
  554.0 11.7 %cholesky.238 = f32[128,128]{1,0:T(8,128)S(1)} custom-call(f32[128,128]{1,0:T(8,128)S(1)} %cholesky.275), custom_call_target="Cholesky" | custom-call | tf_op jit(solution)/shard_map/jit(cholesky)/cholesky | solution.py:33
  565.8 9.8 %custom-call.34 = f32[1,128,128]{1,2,0:T(8,128)S(1)} custom-call(f32[1,128,128]{2,1,0:T(8,128)S(1)} %get-tuple-element.28), custom_call_target="InvertDiagBlocksLowerTriangular" | custom-call | tf_op jit(solution)/shard_map/jit(cholesky)/cholesky | solution.py:33
  575.8 0.4 convolution_subtract_fusion.6
  576.2 11.7 %cholesky.255 = f32[128,128]{1,0:T(8,128)S(1)} custom-call(f32[128,128]{1,0:T(8,128)S(1)} %convolution_subtract_fusion.6), custom_call_target="Cholesky" | custom-call | tf_op jit(solution)/shard_map/jit(cholesky)/cholesky | solution.py:33
  587.9 0.7 compare_reduce_fusion.1
  588.6 0.7 compare_reduce_fusion
  589.3 0.7 compare_reduce_fusion.2
  592.5 0.3 select_select_fusion
  592.9 10.6 %while.1 = (s32[]{:T(128)}, f32[512,512]{1,0:T(8,128)S(1)}, s32[4,2]{0,1:T(2,128)S(1)}, f32[4,128,128]{2,1,0:T(8,128)}, s32[]{:T(128)}) while((s32[]{:T(128)}, f32[512,512]{1,0:T(8,128)S(1)}, s32[4,2]{0,1:T(2,128)S(1)}, f32[4,128,128]{2,1,0:T(8,128)}, s32[]{:T(128)}) %tuple.27), condition=%wide.while_cond, body=%wide.while_body.sunk | while | flops 2 | bytes 132205 | solution.py:10
  592.9 0.6 fusion.76
  593.5 2.0 bitcast_dynamic-update-slice_fusion.18
  595.6 0.6 fusion.76
  596.2 2.0 bitcast_dynamic-update-slice_fusion.18
  598.2 0.6 fusion.76
  598.8 2.0 bitcast_dynamic-update-slice_fusion.18
  600.9 0.6 fusion.76
  601.5 2.0 bitcast_dynamic-update-slice_fusion.18
  603.5 40.1 %custom-call.35 = f32[4,128,128]{1,2,0:T(8,128)S(1)} custom-call(f32[4,128,128]{2,1,0:T(8,128)} %get-tuple-element.12), custom_call_target="InvertDiagBlocksLowerTriangular" | custom-call | tf_op jit(solution)/shard_map/triangular_solve | solution.py:10
  643.6 2.7 fusion.24
  646.3 2.6 convolution_subtract_fusion.1
  648.9 1.3 fusion.52
  650.2 1.5 convolution_subtract_fusion.3
  651.7 1.3 fusion.54
  653.0 2.5 fusion.15
  655.5 1.3 fusion.56
  656.8 1.3 fusion.55
  658.0 1.5 convolution_subtract_fusion
  659.6 1.3 fusion.53
  660.8 1.6 convolution_subtract_fusion.2
  662.4 1.3 fusion.51
  663.7 2.5 fusion.12
  666.2 1.3 fusion.50
  667.4 0.8 fusion.32
  (31 shorter events, 1.4 us)
Async XLA Ops:
  38.5 206.0 %all-to-all-start = ((bf16[16,160,2048]{2,1,0:T(8,128)(2,1)}), bf16[16,160,2048]{2,1,0:T(8,128)(2,1)}, u32[]{:S(2)}, u32[]{:S(2)}) async-start(bf16[16,160,2048]{2,1,0:T(8,128)(2,1)} %bitcast_dynamic-update-slice_fusion.1), calls=%async_computation | async-start | bytes 20971520 | tf_op jit(solution)/shard_map/all_to_all | solution.py:27
  46.9 14.0 %all-gather.2.cloned.1.call-start = ((), (), s32[]{:S(2)}) async-start(), calls=%async_computation.1 | async-start | bytes 3145728 | tf_op jit(solution)/shard_map/all_gather | solution.py:17
  47.6 459.5 %all-reduce.4.cloned.1.call-start = ((), (), s32[]{:S(2)}) async-start(), calls=%async_computation.2 | async-start | bytes 12582912 | tf_op jit(solution)/shard_map/psum | solution.py:36
  60.9 183.7 %copy-start.1 = (bf16[2048,512]{1,0:T(8,128)(2,1)S(1)}, bf16[2048,512]{1,0:T(8,128)(2,1)}, u32[]{:S(2)}) copy-start(bf16[2048,512]{1,0:T(8,128)(2,1)} %all-gather.2.cloned.1.call-done) | copy-start | bytes 6291460
  507.1 1.7 copy-start
  553.6 96.5 %slice-start = ((s8[5242880]{0:T(1024)(128)(4,1)}), s8[1048576]{0:T(1024)(128)(4,1)S(1)}, s32[]{:S(2)}) async-start(s8[5242880]{0:T(1024)(128)(4,1)} %bitcast.93), calls=%async_computation.3 | async-start | bytes 2097152
  643.6 6.6 slice-start.1
Sparse Core Ops, SparseCore 0:
  49.3 11.5 all-gather.1
  255.5 251.5 all-reduce.3
